TPU v7x, 128 devices: a whole 4x4x4 slice. The times are simulated.
128 devices in a mesh: ctx: 8 (over y_hi, x), exp: 16 (over y_lo, z, core).
Axes of the slice: x: 4, y: 4 (y_hi: 2, y_lo: 2; y = y_hi * 2 + y_lo), z: 4, core: 2. Of those that a mesh axis runs over, the one named last changes fastest.
Arguments:
- queries: bfloat16 [16, 1024, 2048], P('exp', 'ctx'), may hold values from -6 to 6
- key_rows: bfloat16 [16, 1024, 256], P('exp', 'ctx'), may hold values from -6 to 6
- value_matrix: bfloat16 [16, 1024, 256], P('exp', 'ctx'), may hold values from -4 to 4
- hidden: bfloat16 [16, 1024, 2880], P('exp', 'ctx'), may hold values from -30 to 30
- out_weight: bfloat16 [2048, 2880], P('ctx'), may hold values from -0.125 to 0.125
- norm_gain: float32 [2880], replicated, may hold values from 0.1 to 1.9
- block_order: int32 [16], replicated, may hold values from 0 to 15, each once
- expert_ids: int32 [16, 1024, 4], P('exp', 'ctx'), may hold values from 0 to 63, all different within a row; in each aligned block of 128 rows (0 to 127, 128 to 255, ..., all dimensions but the last counted through in order) at most 16 rows name the same one
- route_weights: float32 [16, 1024, 4], P('exp', 'ctx'), may hold values from 0.1 to 0.6
- gate_up_weight: bfloat16 [128, 2880, 1440], P(('ctx', 'exp')), may hold values from -0.109375 to 0.109375
- down_weight: bfloat16 [128, 720, 2880], P(('ctx', 'exp')), may hold values from -0.15625 to 0.15625
Outputs:
- layer_out: bfloat16 [16, 1024, 2880], P('exp', 'ctx')
Inputs may be any that keep to these rules, and one draw needn't show every extreme that they name: `expert_ids`: the 128 rows of one device (aligned blocks of rows) name any one expert at most 16 times, a bound that some block reaches.
All inputs are finite; a program needn't handle non-finite values.
Results may differ from a plain program's by a relative error of at most 0.017.
Values may be sent and summed in bfloat16 or wider, within the bound.
A program may use at most 128 MiB of HBM per device.

v0:
```python
import jax
import jax.numpy as jnp
from jax import lax
from jax.sharding import Mesh, PartitionSpec as P

D = 2880
QUERY_HEADS = 32
KEY_VALUE_HEADS = 4
HEAD_SIZE = 64
TOPK = 4
EXPERTS = 64
CAP = 16
CTX = ("y_hi", "x")
EXP = ("y_lo", "z", "core")
CHIPS = ("y_hi", "x", "y_lo", "z")
negative_large = -1e30


def attention(queries, key_rows, value_matrix, block_order):
    token_count = queries.shape[1]
    block_len = token_count // 2
    group = QUERY_HEADS // KEY_VALUE_HEADS
    slot_ids = jnp.arange(16, dtype=jnp.int32)

    def locate(row_index):
        table = (row_index // block_len)[:, None] == slot_ids[None, :]
        return (
            jnp.sum(jnp.where(table, block_order[None, :], 0), axis=1) * block_len
            + row_index % block_len
        )

    query_pos = locate(lax.axis_index(CTX) * token_count + jnp.arange(token_count, dtype=jnp.int32))
    query_head_rows = queries[0].reshape(token_count, KEY_VALUE_HEADS, group, HEAD_SIZE)
    both = lax.all_gather(
        jnp.concatenate([key_rows[0], value_matrix[0]], axis=1), CTX, axis=0, tiled=True
    )
    section_length = both.shape[0]
    key_pos = locate(jnp.arange(section_length, dtype=jnp.int32))
    kv = both.reshape(section_length, 2, KEY_VALUE_HEADS, HEAD_SIZE)
    key_head_rows, value_head_rows = (kv[:, 0], kv[:, 1])
    scores = jnp.einsum(
        "qhgd,khd->hgqk", query_head_rows, key_head_rows, preferred_element_type=jnp.float32
    ) * HEAD_SIZE ** (-0.5)
    visible = key_pos[None, :] <= query_pos[:, None]
    masked = jnp.where(visible, scores, negative_large)
    new_max = jnp.max(masked, axis=-1)
    kept_probs = jnp.where(visible, jnp.exp(masked - new_max[..., None]), 0.0)
    row_total = jnp.sum(kept_probs, axis=-1)
    added = jnp.einsum(
        "hgqk,khd->qhgd",
        kept_probs.astype(jnp.bfloat16),
        value_head_rows,
        preferred_element_type=jnp.float32,
    )
    return (
        (added / jnp.transpose(row_total, (2, 0, 1))[..., None])
        .astype(jnp.bfloat16)
        .reshape(token_count, QUERY_HEADS * HEAD_SIZE)
    )


def local(
    queries,
    key_rows,
    value_matrix,
    hidden,
    out_weight,
    norm_gain,
    block_order,
    expert_ids,
    route_weights,
    gate_up_weight,
    down_weight,
):
    swap = [(0, 1), (1, 0)]
    gate_up_own, down_own = (gate_up_weight[0], down_weight[0])
    gate_up_oth = lax.ppermute(gate_up_own, "core", swap)
    down_oth = lax.ppermute(down_own, "core", swap)
    attended = attention(queries, key_rows, value_matrix, block_order)
    projected = jnp.dot(
        attended,
        lax.all_gather(out_weight, CTX, axis=0, tiled=True),
        preferred_element_type=jnp.float32,
    )
    residual = (hidden[0].astype(jnp.float32) + projected).astype(jnp.bfloat16)
    res_float = residual.astype(jnp.float32)
    moe_in = (
        res_float
        * lax.rsqrt(jnp.mean(res_float * res_float, axis=-1, keepdims=True) + 1e-05)
        * norm_gain
    ).astype(jnp.bfloat16)
    ids, weights = (expert_ids[0], route_weights[0])
    token_count = ids.shape[0]
    named = ids[:, :, None] == jnp.arange(EXPERTS, dtype=jnp.int32)
    member = jnp.any(named, axis=1)
    weight_of = jnp.sum(jnp.where(named, weights[:, :, None], 0.0), axis=1)
    tok = jnp.arange(token_count, dtype=jnp.int32)
    before = (tok[None, :] < tok[:, None]).astype(jnp.bfloat16)
    slot = jnp.dot(before, member.astype(jnp.bfloat16), preferred_element_type=jnp.float32).astype(
        jnp.int32
    )
    place = (
        member.T[:, None, :]
        & (slot.T[:, None, :] == jnp.arange(CAP, dtype=jnp.int32)[None, :, None])
    ).reshape(EXPERTS * CAP, token_count)
    picked = place.astype(jnp.bfloat16)
    spread = jnp.where(
        place,
        jnp.broadcast_to(weight_of.T[:, None, :], (EXPERTS, CAP, token_count)).reshape(
            EXPERTS * CAP, token_count
        ),
        0.0,
    )
    high = spread.astype(jnp.bfloat16)
    low = (spread - high.astype(jnp.float32)).astype(jnp.bfloat16)
    outgoing = jnp.dot(picked, moe_in, preferred_element_type=jnp.float32).astype(jnp.bfloat16)
    rows = lax.all_to_all(
        outgoing.reshape(EXPERTS, CAP, D), CHIPS, split_axis=0, concat_axis=0, tiled=True
    ).reshape(EXPERTS * CAP, D)

    def half(gate_up, down):
        gate_up_out = jnp.dot(rows, gate_up, preferred_element_type=jnp.float32)
        n = gate_up.shape[1] // 2
        gate, up = (gate_up_out[:, :n], gate_up_out[:, n:])
        act = (gate * jax.nn.sigmoid(1.702 * gate) * (up + 1.0)).astype(jnp.bfloat16)
        return jnp.dot(act, down, preferred_element_type=jnp.float32)

    result = (half(gate_up_own, down_own) + half(gate_up_oth, down_oth)).astype(jnp.bfloat16)
    returned = lax.all_to_all(
        result.reshape(EXPERTS, CAP, D), CHIPS, split_axis=0, concat_axis=0, tiled=True
    ).reshape(EXPERTS * CAP, D)
    mixed = jnp.einsum(
        "st,sd->td", high, returned, preferred_element_type=jnp.float32
    ) + jnp.einsum("st,sd->td", low, returned, preferred_element_type=jnp.float32)
    return (res_float + mixed).astype(jnp.bfloat16)[None]


def solution(mesh):
    fine = Mesh(mesh.devices.reshape(2, 4, 2, 4, 2), ("y_hi", "x", "y_lo", "z", "core"))
    rows = P(EXP, CTX, None)
    halves = P(CTX + EXP, None, None)
    return jax.shard_map(
        local,
        mesh=fine,
        in_specs=(rows, rows, rows, rows, P(CTX, None), P(), P(), rows, rows, halves, halves),
        out_specs=rows,
        check_vma=False,
    )
```

profile of v0, /device:TPU:98, one launch (start us, length us, event | category | flops | bytes accessed | tf_op | source)
XLA Modules:
  0.0 508.8 jit_solution(10034185863048073438)
XLA Ops:
  6.5 1.5 pad_maximum_fusion
  8.9 1.3 copy.36
  10.3 0.7 fusion.50
  11.4 0.7 select_reduce_fusion.2
  12.1 0.7 select_reduce_fusion.1
  13.1 45.0 %all-gather.3.cloned.1.call-done = bf16[1024,512]{1,0:T(8,128)(2,1)} async-done(((bf16[128,512]{1,0:T(8,128)(2,1)}), bf16[1024,512]{1,0:T(8,128)(2,1)}) %all-gather.3.cloned.1.call-update) | async-done | bytes 1048592 | tf_op jit(solution)/shard_map/all_gather | solution.py:34
  58.1 1.5 copy.35
  59.5 9.5 %fusion.71 = (f32[4,8,128]{2,1,0:T(8,128)S(1)}, bf16[4,8,128,1024]{2,3,1,0:T(8,128)(2,1)}) fusion(pred[128,1024]{0,1:T(8,128)(4,1)S(1)} %broadcast_compare_fusion, bf16[128,4,8,64]{0,3,2,1:T(8,128)(2,1)S(1)} %bitcast.97, bf16[1024,2,4,64]{0,3,2,1:T(8,128)(2,1)S(1)} %bitcast.95), kind=kOutput, calls=%fused_computation.99 | convolution fusion | flops 562037760 | bytes 9715712 | tf_op jit(solution)/shard_map/sub | solution.py:47
  69.1 5.7 %fusion.32 = bf16[128,4,8,64]{0,3,2,1:T(8,128)(2,1)S(1)} fusion(bf16[4,8,128,1024]{2,3,1,0:T(8,128)(2,1)} %get-tuple-element.6, bf16[1024,2,4,64]{0,3,2,1:T(8,128)(2,1)S(1)} %bitcast.96, f32[128,4,8]{0,2,1:T(8,128)S(1)} %bitcast.111), kind=kOutput, calls=%fused_computation.36 | convolution fusion | flops 537395200 | bytes 9453568 | tf_op jit(solution)/shard_map/hgqk,khd->qhgd/dot_general | solution.py:49
  74.8 139.6 %all-gather.5.cloned.1.call-done = bf16[2048,2880]{0,1:T(8,128)(2,1)} async-done(((bf16[256,2880]{0,1:T(8,128)(2,1)}), bf16[2048,2880]{0,1:T(8,128)(2,1)}) %all-gather.5.cloned.1.call-update) | async-done | bytes 11796496 | tf_op jit(solution)/shard_map/all_gather | solution.py:82
  214.3 6.2 %multiply_reduce_fusion = (f32[128]{0:T(128)S(1)}, f32[128,2880]{0,1:T(8,128)S(1)}) fusion(bf16[2048,2880]{0,1:T(8,128)(2,1)} %all-gather.5.cloned.1.call-done, bf16[128,2048]{0,1:T(8,128)(2,1)S(1)} %bitcast.110, bf16[1,128,2880]{1,2,0:T(8,128)(2,1)S(1)} %copy-done.3), kind=kOutput, calls=%fused_computation.33 | convolution fusion | flops 1512161152 | bytes 14533120 | tf_op jit(solution)/shard_map/dot_general | solution.py:80
  220.5 4.0 convolution_convert_fusion
  224.5 8.5 %copy.38 = bf16[1024,2880]{1,0:T(8,128)(2,1)} copy(bf16[1024,2880]{0,1:T(8,128)(2,1)} %convolution_convert_fusion) | data formatting | bytes 11796480 | tf_op jit(solution)/shard_map/convert_element_type | solution.py:116
  233.1 8.2 %all-to-all-start = ((bf16[64,16,2880]{2,1,0:T(8,128)(2,1)}), bf16[64,16,2880]{2,1,0:T(8,128)(2,1)}, u32[]{:S(2)}, u32[]{:S(2)}) async-start(bf16[64,16,2880]{2,1,0:T(8,128)(2,1)} %bitcast.93), calls=%async_computation | async-start | bytes 12058624 | tf_op jit(solution)/shard_map/all_to_all | solution.py:117
  241.8 88.9 %all-to-all-done = bf16[64,16,2880]{2,1,0:T(8,128)(2,1)} async-done(((bf16[64,16,2880]{2,1,0:T(8,128)(2,1)}), bf16[64,16,2880]{2,1,0:T(8,128)(2,1)}, u32[]{:S(2)}, u32[]{:S(2)}) %all-to-all-start) | async-done | bytes 5898272 | tf_op jit(solution)/shard_map/all_to_all | solution.py:117
  330.7 13.5 %fusion.61 = f32[1024,1440]{0,1:T(8,128)S(1)} fusion(bf16[1024,2880]{1,0:T(8,128)(2,1)} %bitcast.22, bf16[1,2880,1440]{1,2,0:T(8,128)(2,1)} %param.20), kind=kOutput, calls=%fused_computation.89 | convolution fusion | flops 8493465600 | bytes 20090880 | tf_op jit(solution)/shard_map/dot_general | solution.py:122
  344.3 10.0 %fusion.19 = f32[1024,2880]{0,1:T(8,128)} fusion(f32[1024,1440]{0,1:T(8,128)S(1)} %fusion.61, bf16[1,720,2880]{2,1,0:T(8,128)(2,1)} %param.21), kind=kOutput, calls=%fused_computation.27 | convolution fusion | flops 4252631040 | bytes 21841920 | tf_op jit(solution)/shard_map/dot_general | solution.py:126
  354.3 15.1 %fusion.72 = f32[1024,1440]{0,1:T(8,128)} fusion(bf16[1024,2880]{1,0:T(8,128)(2,1)} %bitcast.22, bf16[2880,1440]{0,1:T(8,128)(2,1)} %collective-permute-done), kind=kOutput, calls=%fused_computation.100 | convolution fusion | flops 8493465600 | bytes 20090880 | tf_op jit(solution)/shard_map/dot_general | solution.py:122
  369.4 14.8 %add_convert_fusion = bf16[1024,2880]{0,1:T(8,128)(2,1)} fusion(f32[1024,2880]{0,1:T(8,128)} %fusion.19, bf16[720,2880]{1,0:T(8,128)(2,1)} %collective-permute-done.1, f32[1024,1440]{0,1:T(8,128)} %fusion.72), kind=kOutput, calls=%fused_computation.4 | convolution fusion | flops 4258529280 | bytes 27740160 | tf_op jit(solution)/shard_map/dot_general | solution.py:126
  384.2 8.5 %copy.39 = bf16[1024,2880]{1,0:T(8,128)(2,1)} copy(bf16[1024,2880]{0,1:T(8,128)(2,1)} %add_convert_fusion) | data formatting | bytes 11796480 | tf_op jit(solution)/shard_map/convert_element_type | solution.py:128
  392.7 6.7 %all-to-all-start.1 = ((bf16[64,16,2880]{2,1,0:T(8,128)(2,1)}), bf16[64,16,2880]{2,1,0:T(8,128)(2,1)}, u32[]{:S(2)}, u32[]{:S(2)}) async-start(bf16[64,16,2880]{2,1,0:T(8,128)(2,1)} %bitcast.94), calls=%async_computation.1 | async-start | bytes 12058624 | tf_op jit(solution)/shard_map/all_to_all | solution.py:129
  399.4 91.4 %all-to-all-done.1 = bf16[64,16,2880]{2,1,0:T(8,128)(2,1)} async-done(((bf16[64,16,2880]{2,1,0:T(8,128)(2,1)}), bf16[64,16,2880]{2,1,0:T(8,128)(2,1)}, u32[]{:S(2)}, u32[]{:S(2)}) %all-to-all-start.1) | async-done | bytes 5898272 | tf_op jit(solution)/shard_map/all_to_all | solution.py:129
  490.8 5.2 %convolution_bitcast_fusion = f32[128,2880]{0,1:T(8,128)S(1)} fusion(bf16[64,16,2880]{2,1,0:T(8,128)(2,1)} %all-to-all-done.1, f32[64,128]{1,0:T(8,128)S(1)} %bitcast.98, s32[64,128]{1,0:T(8,128)S(1)} %convolution_convert_fusion.1, pred[64,128]{1,0:T(8,128)(4,1)S(1)} %bitcast.101), kind=kOutput, calls=%fused_computation.11 | convolution fusion | flops 755892224 | bytes 7446528 | tf_op jit(solution)/shard_map/st,sd->td/dot_general | solution.py:134
  496.0 5.9 %fusion.10 = bf16[1,128,2880]{1,2,0:T(8,128)(2,1)} fusion(f32[128,2880]{0,1:T(8,128)S(1)} %get-tuple-element.8, f32[128,2880]{0,1:T(8,128)S(1)} %convolution_bitcast_fusion, bf16[64,16,2880]{2,1,0:T(8,128)(2,1)} %all-to-all-done.1, f32[64,128]{1,0:T(8,128)S(1)} %bitcast.99, s32[64,128]{1,0:T(8,128)S(1)} %convolution_convert_fusion.1, ...), kind=kOutput, calls=%fused_computation.16 | convolution fusion | flops 756473856 | bytes 9658368 | tf_op jit(solution)/shard_map/st,sd->td/dot_general | solution.py:132
  (27 shorter events, 2.1 us)
Async XLA Ops:
  6.5 51.5 %all-gather.3.cloned.1.call-start = ((), (), s32[]{:S(2)}) async-start(), calls=%async_computation.2 | async-start | bytes 1179648 | tf_op jit(solution)/shard_map/all_gather | solution.py:34
  8.1 206.2 %all-gather.5.cloned.1.call-start = ((), (), s32[]{:S(2)}) async-start(), calls=%async_computation.3 | async-start | bytes 13271040 | tf_op jit(solution)/shard_map/all_gather | solution.py:82
  69.1 145.3 %copy-start.3 = (bf16[1,128,2880]{1,2,0:T(8,128)(2,1)S(1)}, bf16[1,128,2880]{1,2,0:T(8,128)(2,1)}, u32[]{:S(2)}) copy-start(bf16[1,128,2880]{1,2,0:T(8,128)(2,1)} %param.14) | copy-start | bytes 2211844
  214.3 6.2 %copy-start = (f32[2880]{0:T(1024)S(1)}, f32[2880]{0:T(1024)}, u32[]{:S(2)}) copy-start(f32[2880]{0:T(1024)} %param.16) | copy-start | bytes 34564
  233.1 97.6 %all-to-all-start = ((bf16[64,16,2880]{2,1,0:T(8,128)(2,1)}), bf16[64,16,2880]{2,1,0:T(8,128)(2,1)}, u32[]{:S(2)}, u32[]{:S(2)}) async-start(bf16[64,16,2880]{2,1,0:T(8,128)(2,1)} %bitcast.93), calls=%async_computation | async-start | bytes 12058624 | tf_op jit(solution)/shard_map/all_to_all | solution.py:117
  241.2 113.1 %collective-permute-start = (bf16[2880,1440]{0,1:T(8,128)(2,1)}, bf16[2880,1440]{0,1:T(8,128)(2,1)}, u32[]{:S(2)}, u32[]{:S(2)}) collective-permute-start(bf16[2880,1440]{0,1:T(8,128)(2,1)} %bitcast.108), channel_id=1, source_target_pairs={{0,1},{1,0},{2,3},{3,2},{4,5},{5,4},{6,7},{7,6},{8,9},{9,8},{10,11... | collective-permute-start | bytes 24883208 | tf_op jit(solution)/shard_map/ppermute | solution.py:77
  241.3 128.1 %collective-permute-start.1 = (bf16[720,2880]{1,0:T(8,128)(2,1)}, bf16[720,2880]{1,0:T(8,128)(2,1)}, u32[]{:S(2)}, u32[]{:S(2)}) collective-permute-start(bf16[720,2880]{1,0:T(8,128)(2,1)} %bitcast.109), channel_id=1, source_target_pairs={{0,1},{1,0},{2,3},{3,2},{4,5},{5,4},{6,7},{7,6},{8,9},{9,8},{10,11... | collective-permute-start | bytes 12441608 | tf_op jit(solution)/shard_map/ppermute | solution.py:78
  392.7 6.7 %copy-start.1 = (s32[1,128,4]{1,2,0:T(4,128)S(1)}, s32[1,128,4]{1,2,0:T(4,128)}, u32[]{:S(2)}) copy-start(s32[1,128,4]{1,2,0:T(4,128)} %param.18) | copy-start | bytes 6148
  392.7 6.7 %copy-start.2 = (f32[1,128,4]{1,2,0:T(4,128)S(1)}, f32[1,128,4]{1,2,0:T(4,128)}, u32[]{:S(2)}) copy-start(f32[1,128,4]{1,2,0:T(4,128)} %param.19) | copy-start | bytes 6148
  392.7 98.1 %all-to-all-start.1 = ((bf16[64,16,2880]{2,1,0:T(8,128)(2,1)}), bf16[64,16,2880]{2,1,0:T(8,128)(2,1)}, u32[]{:S(2)}, u32[]{:S(2)}) async-start(bf16[64,16,2880]{2,1,0:T(8,128)(2,1)} %bitcast.94), calls=%async_computation.1 | async-start | bytes 12058624 | tf_op jit(solution)/shard_map/all_to_all | solution.py:129
Sparse Core Ops, SparseCore 0:
  9.7 48.3 all-gather.2
  60.2 154.0 all-gather.4
where the time goes:
time: 510 us; the launch traced here: 509 us
  waiting for transfers between devices  366 us (72%)
  matrix products  90.2 us (18%)
  local copies, waits for them, and re-layouts  19.9 us (4%)
  starting transfers between devices  15.5 us (3%)
  between operations  13.6 us (3%)
    all_gather x1, waiting for transfers between devices, local(): lax.all_gather(out_weight, CTX, axis=0, tiled=True)  140 us
    all_to_all x1, waiting for transfers between devices, local(): lax.all_to_all(result.reshape(EXPERTS, CAP, D), CHIPS, split_axis=0, conc...  91.4 us
    all_to_all x1, waiting for transfers between devices, local(): lax.all_to_all(outgoing.reshape(EXPERTS, CAP, D), CHIPS, split_axis=0, co...  88.9 us
    all_gather x1, waiting for transfers between devices, attention(): lax.all_gather(jnp.concatenate([key_rows[0], value_matrix[0]], axis=1), C...  45 us
    dot_general x2, matrix products, half(): gate_up_out = jnp.dot(rows, gate_up, preferred_element_type=jnp.float32)  28.7 us
    dot_general x2, matrix products, half(): return jnp.dot(act, down, preferred_element_type=jnp.float32)  24.8 us
  transfers between devices with their start and end apart: 6, of which 4 were waited for; matrix products, arithmetic and copies ran while one was open for 12% of the time, Pallas kernels for 0%

commit v1 on v0

--- a/solution.py
+++ b/solution.py
@@ -79,7 +79,9 @@
     attended = attention(queries, key_rows, value_matrix, block_order)
     projected = jnp.dot(
         attended,
-        lax.all_gather(out_weight, CTX, axis=0, tiled=True),
+        jnp.concatenate(
+            lax.all_to_all(jnp.stack([out_weight] * lax.axis_size(CTX)), CTX, 0, 0), axis=0
+        ),
         preferred_element_type=jnp.float32,
     )
     residual = (hidden[0].astype(jnp.float32) + projected).astype(jnp.bfloat16)

time: 510 us -> 529 us (1.037)
  waiting for transfers between devices: 366 us -> 337 us
  starting transfers between devices: 15.5 us -> 43.9 us
  local copies, waits for them, and re-layouts: 19.9 us -> 41.6 us
    all_gather x1 -> x0, waiting for transfers between devices: 140 us -> none  [local(): lax.all_gather(out_weight, CTX, axis=0, tiled=True)]
    all_gather x1, waiting for transfers between devices: 45 us -> 158 us  [attention(): lax.all_gather(jnp.concatenate([key_rows[0], value_matrix[0]], axis=1), C...]
    all_to_all x1, starting transfers between devices: 8.18 us -> 29 us  [local(): lax.all_to_all(outgoing.reshape(EXPERTS, CAP, D), CHIPS, split_axis=0, co...]
    all_to_all x0 -> x1, local copies, waits for them, and re-layouts: none -> 16.2 us  [local(): lax.all_to_all(jnp.stack([out_weight] * lax.axis_size(CTX)), CTX, 0, 0)]
    all_to_all x0 -> x1, starting transfers between devices: none -> 7.6 us  [local(): lax.all_to_all(jnp.stack([out_weight] * lax.axis_size(CTX)), CTX, 0, 0)]
    another operation x0 -> x1, local copies, waits for them, and re-layouts: none -> 6.55 us  [local(): jnp.stack([out_weight] * lax.axis_size(CTX))]
  transfers between devices with their start and end apart: 6 -> 6, of which waited for: 4 -> 4; matrix products, arithmetic and copies ran while one was open for 12% -> 11% of each run, Pallas kernels for 0% -> 0%
where the time goes in v1:
time: 529 us; the launch traced here: 528 us
  waiting for transfers between devices  337 us (64%)
  matrix products  90.4 us (17%)
  starting transfers between devices  43.9 us (8%)
  local copies, waits for them, and re-layouts  41.6 us (8%)
  between operations  13.6 us (3%)
    all_gather x1, waiting for transfers between devices, attention(): lax.all_gather(jnp.concatenate([key_rows[0], value_matrix[0]], axis=1), C...  158 us
    all_to_all x1, waiting for transfers between devices, local(): lax.all_to_all(result.reshape(EXPERTS, CAP, D), CHIPS, split_axis=0, conc...  88.8 us
    all_to_all x1, waiting for transfers between devices, local(): lax.all_to_all(outgoing.reshape(EXPERTS, CAP, D), CHIPS, split_axis=0, co...  87.7 us
    all_to_all x1, starting transfers between devices, local(): lax.all_to_all(outgoing.reshape(EXPERTS, CAP, D), CHIPS, split_axis=0, co...  29 us
    dot_general x2, matrix products, half(): gate_up_out = jnp.dot(rows, gate_up, preferred_element_type=jnp.float32)  28.7 us
    dot_general x2, matrix products, half(): return jnp.dot(act, down, preferred_element_type=jnp.float32)  24.8 us
    all_to_all x1, local copies, waits for them, and re-layouts, local(): lax.all_to_all(jnp.stack([out_weight] * lax.axis_size(CTX)), CTX, 0, 0)  16.2 us
  transfers between devices with their start and end apart: 6, of which 4 were waited for; matrix products, arithmetic and copies ran while one was open for 11% of the time, Pallas kernels for 0%

profile of v1, /device:TPU:98, one launch (start us, length us, event | category | flops | bytes accessed | tf_op | source)
XLA Modules:
  0.0 527.6 jit_solution(5914609427373871652)
XLA Ops:
  6.5 6.5 %stack.2 = bf16[8,256,2880]{1,2,0:T(8,128)(2,1)} broadcast(bf16[256,2880]{0,1:T(8,128)(2,1)} %param.15), dimensions={1,2} | broadcast | bytes 13271040 | tf_op jit(solution)/shard_map/stack | solution.py:83
  13.1 7.6 %all-to-all-start = ((bf16[8,256,2880]{1,2,0:T(8,128)(2,1)}), bf16[8,256,2880]{1,2,0:T(8,128)(2,1)}, u32[]{:S(2)}, u32[]{:S(2)}) async-start(bf16[8,256,2880]{1,2,0:T(8,128)(2,1)} %stack.2), calls=%async_computation | async-start | bytes 23592960 | tf_op jit(solution)/shard_map/all_to_all | solution.py:83
  20.7 0.7 pad_maximum_fusion
  22.7 158.2 %all-gather.2.cloned.1.call-done = bf16[1024,512]{1,0:T(8,128)(2,1)} async-done(((bf16[128,512]{1,0:T(8,128)(2,1)}), bf16[1024,512]{1,0:T(8,128)(2,1)}) %all-gather.2.cloned.1.call-update) | async-done | bytes 1048592 | tf_op jit(solution)/shard_map/all_gather | solution.py:34
  180.8 1.5 copy.45
  182.3 9.6 %fusion.71 = (f32[4,8,128]{2,1,0:T(8,128)S(1)}, bf16[4,8,128,1024]{2,3,1,0:T(8,128)(2,1)}) fusion(pred[128,1024]{0,1:T(8,128)(4,1)S(1)} %broadcast_compare_fusion, bf16[128,4,8,64]{0,3,2,1:T(8,128)(2,1)S(1)} %bitcast.100, bf16[1024,2,4,64]{0,3,2,1:T(8,128)(2,1)S(1)} %bitcast.97), kind=kOutput, calls=%fused_computation.99 | convolution fusion | flops 562037760 | bytes 9715712 | tf_op jit(solution)/shard_map/sub | solution.py:47
  192.0 4.9 fusion.32
  196.9 2.0 all-to-all-done
  198.9 16.2 %copy.48 = bf16[8,256,2880]{2,1,0:T(8,128)(2,1)} copy(bf16[8,256,2880]{1,2,0:T(8,128)(2,1)} %all-to-all-done) | data formatting | bytes 23592960 | tf_op jit(solution)/shard_map/all_to_all | solution.py:83
  215.2 7.1 %multiply_reduce_fusion = (f32[128]{0:T(128)S(1)}, f32[128,2880]{0,1:T(8,128)S(1)}) fusion(bf16[128,2048]{0,1:T(8,128)(2,1)S(1)} %bitcast.99, bf16[2048,2880]{1,0:T(8,128)(2,1)} %bitcast.94, bf16[1,128,2880]{1,2,0:T(8,128)(2,1)S(1)} %copy-done), kind=kOutput, calls=%fused_computation.33 | convolution fusion | flops 1512161152 | bytes 14533120 | tf_op jit(solution)/shard_map/dot_general | solution.py:80
  222.3 4.0 convolution_convert_fusion
  226.3 8.5 %copy.49 = bf16[1024,2880]{1,0:T(8,128)(2,1)} copy(bf16[1024,2880]{0,1:T(8,128)(2,1)} %convolution_convert_fusion) | data formatting | bytes 11796480 | tf_op jit(solution)/shard_map/convert_element_type | solution.py:118
  234.8 29.0 %all-to-all-start.1 = ((bf16[64,16,2880]{2,1,0:T(8,128)(2,1)}), bf16[64,16,2880]{2,1,0:T(8,128)(2,1)}, u32[]{:S(2)}, u32[]{:S(2)}) async-start(bf16[64,16,2880]{2,1,0:T(8,128)(2,1)} %bitcast.95), calls=%async_computation.1 | async-start | bytes 12058624 | tf_op jit(solution)/shard_map/all_to_all | solution.py:119
  263.9 0.5 collective-permute-start.1
  264.4 87.7 %all-to-all-done.1 = bf16[64,16,2880]{2,1,0:T(8,128)(2,1)} async-done(((bf16[64,16,2880]{2,1,0:T(8,128)(2,1)}), bf16[64,16,2880]{2,1,0:T(8,128)(2,1)}, u32[]{:S(2)}, u32[]{:S(2)}) %all-to-all-start.1) | async-done | bytes 5898272 | tf_op jit(solution)/shard_map/all_to_all | solution.py:119
  352.1 13.5 %fusion.61 = f32[1024,1440]{0,1:T(8,128)S(1)} fusion(bf16[1024,2880]{1,0:T(8,128)(2,1)} %bitcast.23, bf16[1,2880,1440]{1,2,0:T(8,128)(2,1)} %param.20), kind=kOutput, calls=%fused_computation.89 | convolution fusion | flops 8493465600 | bytes 20090880 | tf_op jit(solution)/shard_map/dot_general | solution.py:124
  365.7 10.0 %fusion.19 = f32[1024,2880]{0,1:T(8,128)} fusion(f32[1024,1440]{0,1:T(8,128)S(1)} %fusion.61, bf16[1,720,2880]{2,1,0:T(8,128)(2,1)} %param.21), kind=kOutput, calls=%fused_computation.27 | convolution fusion | flops 4252631040 | bytes 21841920 | tf_op jit(solution)/shard_map/dot_general | solution.py:128
  375.7 15.1 %fusion.72 = f32[1024,1440]{0,1:T(8,128)} fusion(bf16[1024,2880]{1,0:T(8,128)(2,1)} %bitcast.23, bf16[2880,1440]{0,1:T(8,128)(2,1)} %collective-permute-done), kind=kOutput, calls=%fused_computation.100 | convolution fusion | flops 8493465600 | bytes 20090880 | tf_op jit(solution)/shard_map/dot_general | solution.py:124
  390.8 14.8 %add_convert_fusion = bf16[1024,2880]{0,1:T(8,128)(2,1)} fusion(f32[1024,2880]{0,1:T(8,128)} %fusion.19, bf16[720,2880]{1,0:T(8,128)(2,1)} %collective-permute-done.1, f32[1024,1440]{0,1:T(8,128)} %fusion.72), kind=kOutput, calls=%fused_computation.4 | convolution fusion | flops 4258529280 | bytes 27740160 | tf_op jit(solution)/shard_map/dot_general | solution.py:128
  405.6 8.5 %copy.50 = bf16[1024,2880]{1,0:T(8,128)(2,1)} copy(bf16[1024,2880]{0,1:T(8,128)(2,1)} %add_convert_fusion) | data formatting | bytes 11796480 | tf_op jit(solution)/shard_map/convert_element_type | solution.py:130
  414.1 6.7 %all-to-all-start.2 = ((bf16[64,16,2880]{2,1,0:T(8,128)(2,1)}), bf16[64,16,2880]{2,1,0:T(8,128)(2,1)}, u32[]{:S(2)}, u32[]{:S(2)}) async-start(bf16[64,16,2880]{2,1,0:T(8,128)(2,1)} %bitcast.96), calls=%async_computation.2 | async-start | bytes 12058624 | tf_op jit(solution)/shard_map/all_to_all | solution.py:131
  420.8 88.8 %all-to-all-done.2 = bf16[64,16,2880]{2,1,0:T(8,128)(2,1)} async-done(((bf16[64,16,2880]{2,1,0:T(8,128)(2,1)}), bf16[64,16,2880]{2,1,0:T(8,128)(2,1)}, u32[]{:S(2)}, u32[]{:S(2)}) %all-to-all-start.2) | async-done | bytes 5898272 | tf_op jit(solution)/shard_map/all_to_all | solution.py:131
  509.6 5.2 convolution_bitcast_fusion
  514.8 5.9 %fusion.12 = bf16[1,128,2880]{1,2,0:T(8,128)(2,1)} fusion(f32[128,2880]{0,1:T(8,128)S(1)} %get-tuple-element.8, f32[128,2880]{0,1:T(8,128)S(1)} %convolution_bitcast_fusion, bf16[64,16,2880]{2,1,0:T(8,128)(2,1)} %all-to-all-done.2, f32[64,128]{1,0:T(8,128)S(1)} %bitcast.102, s32[64,128]{1,0:T(8,128)S(1)} %convolution_convert_fusion.1, ...), kind=kOutput, calls=%fused_computation.19 | convolution fusion | flops 756473856 | bytes 9658368 | tf_op jit(solution)/shard_map/st,sd->td/dot_general | solution.py:134
  (36 shorter events, 1.3 us)
Async XLA Ops:
  13.1 7.6 %copy-start.2 = (bf16[1,128,256]{2,1,0:T(8,128)(2,1)S(1)}, bf16[1,128,256]{2,1,0:T(8,128)(2,1)}, u32[]{:S(2)}) copy-start(bf16[1,128,256]{2,1,0:T(8,128)(2,1)} %param.13) | copy-start | bytes 196612
  13.1 7.6 %copy-start.3 = (bf16[1,128,256]{2,1,0:T(8,128)(2,1)S(1)}, bf16[1,128,256]{2,1,0:T(8,128)(2,1)}, u32[]{:S(2)}) copy-start(bf16[1,128,256]{2,1,0:T(8,128)(2,1)} %param.12) | copy-start | bytes 196612
  13.1 8.4 %copy-start.1 = (bf16[1,128,2048]{2,1,0:T(8,128)(2,1)S(1)}, bf16[1,128,2048]{2,1,0:T(8,128)(2,1)}, u32[]{:S(2)}) copy-start(bf16[1,128,2048]{2,1,0:T(8,128)(2,1)} %param.11) | copy-start | bytes 1572868
  13.1 8.7 %copy-start.5 = (s32[1,128,4]{1,2,0:T(4,128)S(1)}, s32[1,128,4]{1,2,0:T(4,128)}, u32[]{:S(2)}) copy-start(s32[1,128,4]{1,2,0:T(4,128)} %param.18) | copy-start | bytes 6148
  13.1 9.1 %copy-start.7 = (s32[16]{0:T(128)S(1)}, s32[16]{0:T(128)}, u32[]{:S(2)}) copy-start(s32[16]{0:T(128)} %param.17) | copy-start | bytes 196
  13.1 185.8 %all-to-all-start = ((bf16[8,256,2880]{1,2,0:T(8,128)(2,1)}), bf16[8,256,2880]{1,2,0:T(8,128)(2,1)}, u32[]{:S(2)}, u32[]{:S(2)}) async-start(bf16[8,256,2880]{1,2,0:T(8,128)(2,1)} %stack.2), calls=%async_computation | async-start | bytes 23592960 | tf_op jit(solution)/shard_map/all_to_all | solution.py:83
  20.7 160.1 %all-gather.2.cloned.1.call-start = ((), (), s32[]{:S(2)}) async-start(), calls=%async_computation.3 | async-start | bytes 1179648 | tf_op jit(solution)/shard_map/all_gather | solution.py:34
  196.9 18.2 %copy-start = (bf16[1,128,2880]{1,2,0:T(8,128)(2,1)S(1)}, bf16[1,128,2880]{1,2,0:T(8,128)(2,1)}, u32[]{:S(2)}) copy-start(bf16[1,128,2880]{1,2,0:T(8,128)(2,1)} %param.14) | copy-start | bytes 2211844
  215.2 7.1 %copy-start.4 = (f32[2880]{0:T(1024)S(1)}, f32[2880]{0:T(1024)}, u32[]{:S(2)}) copy-start(f32[2880]{0:T(1024)} %param.16) | copy-start | bytes 34564
  234.8 117.3 %all-to-all-start.1 = ((bf16[64,16,2880]{2,1,0:T(8,128)(2,1)}), bf16[64,16,2880]{2,1,0:T(8,128)(2,1)}, u32[]{:S(2)}, u32[]{:S(2)}) async-start(bf16[64,16,2880]{2,1,0:T(8,128)(2,1)} %bitcast.95), calls=%async_computation.1 | async-start | bytes 12058624 | tf_op jit(solution)/shard_map/all_to_all | solution.py:119
  263.8 111.8 %collective-permute-start = (bf16[2880,1440]{0,1:T(8,128)(2,1)}, bf16[2880,1440]{0,1:T(8,128)(2,1)}, u32[]{:S(2)}, u32[]{:S(2)}) collective-permute-start(bf16[2880,1440]{0,1:T(8,128)(2,1)} %bitcast.111), channel_id=1, source_target_pairs={{0,1},{1,0},{2,3},{3,2},{4,5},{5,4},{6,7},{7,6},{8,9},{9,8},{10,11... | collective-permute-start | bytes 24883208 | tf_op jit(solution)/shard_map/ppermute | solution.py:77
  263.9 126.9 %collective-permute-start.1 = (bf16[720,2880]{1,0:T(8,128)(2,1)}, bf16[720,2880]{1,0:T(8,128)(2,1)}, u32[]{:S(2)}, u32[]{:S(2)}) collective-permute-start(bf16[720,2880]{1,0:T(8,128)(2,1)} %bitcast.112), channel_id=1, source_target_pairs={{0,1},{1,0},{2,3},{3,2},{4,5},{5,4},{6,7},{7,6},{8,9},{9,8},{10,11... | collective-permute-start | bytes 12441608 | tf_op jit(solution)/shard_map/ppermute | solution.py:78
  414.1 6.7 %copy-start.6 = (f32[1,128,4]{1,2,0:T(4,128)S(1)}, f32[1,128,4]{1,2,0:T(4,128)}, u32[]{:S(2)}) copy-start(f32[1,128,4]{1,2,0:T(4,128)} %param.19) | copy-start | bytes 6148
  414.1 95.5 %all-to-all-start.2 = ((bf16[64,16,2880]{2,1,0:T(8,128)(2,1)}), bf16[64,16,2880]{2,1,0:T(8,128)(2,1)}, u32[]{:S(2)}, u32[]{:S(2)}) async-start(bf16[64,16,2880]{2,1,0:T(8,128)(2,1)} %bitcast.96), calls=%async_computation.2 | async-start | bytes 12058624 | tf_op jit(solution)/shard_map/all_to_all | solution.py:131
Sparse Core Ops, SparseCore 0:
  23.9 156.9 all-gather.1
